TPU v7x, 32 devices: a whole 2x2x4 slice. The times are simulated.
32 devices in a mesh: seq: 16 (over z, x, core), head: 2 (over y).
Axes of the slice: x: 2, y: 2, z: 4, core: 2. Of those that a mesh axis runs over, the one named last changes fastest.
Arguments:
- alignment_rows: bfloat16 [128, 1024, 256], P('seq'), may hold values from -16 to 16
- upstream_derivative_tensor: bfloat16 [128, 1024, 256], P(None, 'seq'), may hold values from -12 to 12
- saved_pair_bias: bfloat16 [8, 1024, 1024], P('head', 'seq'), may hold values from -360 to 360
- pairwise_features: bfloat16 [1024, 1024, 128], P('seq', 'head'), may hold values from -16 to 16
- sequence_layernorm_scaling: float32 [256], replicated, may hold values from 0.5 to 2
- sequence_layernorm_centre: float32 [256], replicated, may hold values from -1 to 1
- asking_projection_matrix: bfloat16 [256, 256], replicated, may hold values from -0.375 to 0.375
- matching_projection_matrix: bfloat16 [256, 256], replicated, may hold values from -0.375 to 0.375
- content_projection_matrix: bfloat16 [256, 256], replicated, may hold values from -0.375 to 0.375
- sigmoid_projection_matrix: bfloat16 [256, 256], replicated, may hold values from -0.375 to 0.375
- gate_offset_bias: float32 [256], replicated, may hold values from -2 to 2
- final_projection_matrix: bfloat16 [256, 256], replicated, may hold values from -0.375 to 0.375
- pairwise_norm_gain: float32 [128], replicated, may hold values from 0.5 to 2
- pairwise_weight: bfloat16 [128, 8], replicated, may hold values from -0.5 to 0.5
Outputs:
- alignment_input_gradient: bfloat16 [128, 1024, 256], P('seq', 'head')
- pairwise_gradient: bfloat16 [1024, 1024, 128], P('seq', 'head')
All inputs are finite; a program needn't handle non-finite values.
Results may differ from a plain program's by a relative error of at most 0.012.
The roundings to bfloat16 on the way count: a program that leaves them out, or rounds other values in their place, can miss the bound.
Values may be sent and summed in bfloat16 or wider, within the bound.
A program may use at most 320 MiB of HBM per device.

v0:
```python
import jax
import jax.numpy as jnp
from jax import lax
from jax.sharding import PartitionSpec as P

SUBSPACE_WIDTH = 32
epsilon = 1e-05


def layer_statistics(values):
    average = jnp.mean(values, axis=-1, keepdims=True)
    centred = values - average
    inverse_deviation = lax.rsqrt(jnp.mean(centred * centred, axis=-1, keepdims=True) + epsilon)
    return (centred * inverse_deviation, inverse_deviation)


def layer_reverse_step(upstream, standardized_values, inverse_deviation):
    first_mean = jnp.mean(upstream, axis=-1, keepdims=True)
    second_mean = jnp.mean(upstream * standardized_values, axis=-1, keepdims=True)
    return inverse_deviation * (upstream - first_mean - standardized_values * second_mean)


def per_device(
    alignment_rows,
    upstream_derivative_tensor,
    saved_pair_bias,
    pairwise_features,
    sequence_layernorm_scaling,
    sequence_layernorm_centre,
    asking_projection_matrix,
    matching_projection_matrix,
    content_projection_matrix,
    sigmoid_projection_matrix,
    gate_offset_bias,
    final_projection_matrix,
    pairwise_norm_gain,
    pairwise_weight,
):
    local_heads = saved_pair_bias.shape[0]
    all_heads = pairwise_weight.shape[1]
    resident_rows, residue_total, channel_count = alignment_rows.shape
    head_width = local_heads * SUBSPACE_WIDTH
    first_head = lax.axis_index("head") * local_heads
    first_col = first_head * SUBSPACE_WIDTH
    score_scale = SUBSPACE_WIDTH ** (-0.5)
    bias_full = lax.all_gather(saved_pair_bias, "seq", axis=1, tiled=True)
    standardized_values, inverse_deviation = layer_statistics(alignment_rows.astype(jnp.float32))
    normalized_rows = (
        standardized_values * sequence_layernorm_scaling + sequence_layernorm_centre
    ).astype(jnp.bfloat16)

    def project(coefficient_matrix):
        columns = lax.dynamic_slice_in_dim(coefficient_matrix, first_col, head_width, 1)
        return jnp.dot(normalized_rows, columns, preferred_element_type=jnp.float32)

    head_shape = (resident_rows, residue_total, local_heads, SUBSPACE_WIDTH)
    query = (
        (score_scale * project(asking_projection_matrix)).astype(jnp.bfloat16).reshape(head_shape)
    )
    keys_all = project(matching_projection_matrix).astype(jnp.bfloat16).reshape(head_shape)
    vals_all = project(content_projection_matrix).astype(jnp.bfloat16).reshape(head_shape)
    gate_shift = lax.dynamic_slice_in_dim(gate_offset_bias, first_col, head_width, 0)
    gate = jax.nn.sigmoid(project(sigmoid_projection_matrix) + gate_shift).reshape(head_shape)
    out_rows = lax.dynamic_slice_in_dim(final_projection_matrix, first_col, head_width, 0)
    row_grads = lax.all_to_all(
        upstream_derivative_tensor, "seq", split_axis=0, concat_axis=1, tiled=True
    )
    gated_grad = jnp.einsum(
        "src,wc->srw", row_grads, out_rows, preferred_element_type=jnp.float32
    ).astype(jnp.bfloat16)
    gated_grad = gated_grad.reshape(head_shape)
    bias_float = bias_full.astype(jnp.float32)

    def row_reverse_step(pair_bias_gradient, layer_inputs):
        query_row, keys_row, vals_row, gate_row, row_gradient = layer_inputs
        logits = (
            jnp.einsum("ihd,jhd->hij", query_row, keys_row, preferred_element_type=jnp.float32)
            + bias_float
        )
        probs = jax.nn.softmax(logits, axis=-1)
        probs_low = probs.astype(jnp.bfloat16)
        attended = jnp.einsum(
            "hij,jhd->ihd", probs_low, vals_row, preferred_element_type=jnp.float32
        )
        grad_float = row_gradient.astype(jnp.float32)
        attended_grad = (grad_float * gate_row).astype(jnp.bfloat16)
        gate_grad = (grad_float * attended * gate_row * (1.0 - gate_row)).astype(jnp.bfloat16)
        prob_grad = jnp.einsum(
            "ihd,jhd->hij", attended_grad, vals_row, preferred_element_type=jnp.float32
        )
        inner_sum = jnp.sum(probs * prob_grad, axis=-1, keepdims=True)
        score_grad = probs * (prob_grad - inner_sum)
        score_low = score_grad.astype(jnp.bfloat16)
        query_grad = (
            score_scale
            * jnp.einsum("hij,jhd->ihd", score_low, keys_row, preferred_element_type=jnp.float32)
        ).astype(jnp.bfloat16)
        key_grad = jnp.einsum(
            "hij,ihd->jhd", score_low, query_row, preferred_element_type=jnp.float32
        ).astype(jnp.bfloat16)
        value_grad = jnp.einsum(
            "hij,ihd->jhd", probs_low, attended_grad, preferred_element_type=jnp.float32
        ).astype(jnp.bfloat16)
        grads = jnp.concatenate([query_grad, key_grad, value_grad, gate_grad], axis=-1)
        return (pair_bias_gradient + score_grad, grads)

    pair_bias_gradient, head_grad_rows = lax.scan(
        row_reverse_step,
        jnp.zeros((local_heads, residue_total, residue_total), jnp.float32),
        (query, keys_all, vals_all, gate, gated_grad),
    )
    piled_arrays = jnp.stack(
        [
            coefficient_matrix.reshape(channel_count, all_heads, SUBSPACE_WIDTH)
            for coefficient_matrix in (
                asking_projection_matrix,
                matching_projection_matrix,
                content_projection_matrix,
                sigmoid_projection_matrix,
            )
        ],
        axis=2,
    )
    piled_arrays = piled_arrays.reshape(channel_count, all_heads, 4 * SUBSPACE_WIDTH)
    local_weight = lax.dynamic_slice_in_dim(piled_arrays, first_head, local_heads, 1)
    partial_term = jnp.einsum(
        "srhf,chf->src", head_grad_rows, local_weight, preferred_element_type=jnp.float32
    )
    normalized_gradient = lax.psum_scatter(
        partial_term.astype(jnp.bfloat16), "head", scatter_dimension=1, tiled=True
    ).astype(jnp.float32)
    block_len = residue_total // lax.axis_size("head")
    block_start = lax.axis_index("head") * block_len
    normalized_block = lax.dynamic_slice_in_dim(standardized_values, block_start, block_len, 1)
    inverse_spread_block = lax.dynamic_slice_in_dim(inverse_deviation, block_start, block_len, 1)
    alignment_input_gradient = layer_reverse_step(
        normalized_gradient * sequence_layernorm_scaling, normalized_block, inverse_spread_block
    ).astype(jnp.bfloat16)
    summed_rows = lax.psum_scatter(pair_bias_gradient, "seq", scatter_dimension=1, tiled=True)
    bias_tile = lax.all_to_all(
        summed_rows.astype(jnp.bfloat16), "head", split_axis=2, concat_axis=0, tiled=True
    ).astype(summed_rows.dtype)
    bias_low = bias_tile.astype(jnp.bfloat16)
    pair_hat, pair_inv = layer_statistics(pairwise_features.astype(jnp.float32))
    pair_normed_grad = jnp.einsum(
        "hij,ch->ijc", bias_low, pairwise_weight, preferred_element_type=jnp.float32
    )
    pairwise_gradient = layer_reverse_step(
        pair_normed_grad * pairwise_norm_gain, pair_hat, pair_inv
    ).astype(jnp.bfloat16)
    return (alignment_input_gradient, pairwise_gradient)


def solution(mesh):
    placed = (
        P("seq", None, None),
        P(None, "seq", None),
        P("head", "seq", None),
        P("seq", "head", None),
        P(),
        P(),
        P(),
        P(),
        P(),
        P(),
        P(),
        P(),
        P(),
        P(),
    )
    return jax.shard_map(
        per_device,
        mesh=mesh,
        in_specs=placed,
        out_specs=(P("seq", "head", None), P("seq", "head", None)),
        check_vma=False,
    )
```

profile of v0, /device:TPU:10, one launch (start us, length us, event | category | flops | bytes accessed | tf_op | source)
XLA Modules:
  0.0 1453.9 jit_solution(13815604666751804673)
XLA Ops:
  66.9 91.8 %all-to-all-done = bf16[128,64,256]{2,1,0:T(8,128)(2,1)} async-done(((bf16[128,64,256]{2,1,0:T(8,128)(2,1)}), bf16[128,64,256]{2,1,0:T(8,128)(2,1)}, u32[]{:S(2)}, u32[]{:S(2)}) %all-to-all-start) | async-done | bytes 4194336 | tf_op jit(solution)/shard_map/all_to_all | solution.py:65
  164.0 15.8 %copy.64 = f32[4,1024,1024]{1,2,0:T(8,128)} copy(bf16[4,1024,1024]{2,0,1:T(4,128)(2,1)} %all-gather.2.cloned.1.call-done) | data formatting | bytes 25165824
  179.9 820.5 %while.13 = (s32[]{:T(128)}, f32[4,1024,1024]{1,2,0:T(8,128)}, bf16[8,1024,4,128]{1,3,2,0:T(8,128)(2,1)}, bf16[8,1024,4,32]{1,3,2,0:T(8,128)(2,1)}, bf16[8,1024,...) while((s32[]{:T(128)}, f32[4,1024,1024]{1,2,0:T(8,128)}, ...), condition=%wide.region_6.7_spmd.clone, body=%wide.region_2.6_spmd.clone.sunk | while | flops 1692408832 | bytes 267244176 | solution.py:107
  203.9 18.6 %fusion.127 = (f32[4,1024]{1,0:T(4,128)S(1)}, f32[4,1024,1024]{1,2,0:T(8,128)}) fusion(f32[4,1024,1024]{1,2,0:T(8,128)} %convolution_add_fusion.2), kind=kOutput, calls=%fused_computation.106.clone.1 | output fusion | flops 8389631 | bytes 33570816 | tf_op jit(solution)/shard_map/while/body/eval_jaxpr/sub | solution.py:80
  236.8 17.3 %fusion.128 = (bf16[4,1024,1024]{1,2,0:T(8,128)(2,1)S(1)}, f32[4,1024,1024]{1,2,0:T(8,128)}) fusion(f32[4,1024,1024]{1,2,0:T(8,128)} %get-tuple-element.193, f32[4,1024]{1,0:T(4,128)S(1)} %get-tuple-element.194, f32[4,1024,1024]{1,2,0:T(8,128)} %get-tuple-element.191, f32[4,1024]{1,0:T(4,128)S(1)} %get-tuple-element.192, ...), kind=kLoop, calls=%fused_computation.7.clone.1 | loop fusion | flops 25165824 | bytes 75530240 | tf_op jit(solution)/shard_map/while/body/eval_jaxpr/convert_element_type | solution.py:93
  299.9 18.6 %fusion.127 = (f32[4,1024]{1,0:T(4,128)S(1)}, f32[4,1024,1024]{1,2,0:T(8,128)}) fusion(f32[4,1024,1024]{1,2,0:T(8,128)} %convolution_add_fusion.2), kind=kOutput, calls=%fused_computation.106.clone.1 | output fusion | flops 8389631 | bytes 33570816 | tf_op jit(solution)/shard_map/while/body/eval_jaxpr/sub | solution.py:80
  318.5 14.3 multiply_reduce_fusion.4
  332.8 23.3 %fusion.128 = (bf16[4,1024,1024]{1,2,0:T(8,128)(2,1)S(1)}, f32[4,1024,1024]{1,2,0:T(8,128)}) fusion(f32[4,1024,1024]{1,2,0:T(8,128)} %get-tuple-element.193, f32[4,1024]{1,0:T(4,128)S(1)} %get-tuple-element.194, f32[4,1024,1024]{1,2,0:T(8,128)} %get-tuple-element.191, f32[4,1024]{1,0:T(4,128)S(1)} %get-tuple-element.192, ...), kind=kLoop, calls=%fused_computation.7.clone.1 | loop fusion | flops 25165824 | bytes 75530240 | tf_op jit(solution)/shard_map/while/body/eval_jaxpr/convert_element_type | solution.py:93
  402.0 18.6 %fusion.127 = (f32[4,1024]{1,0:T(4,128)S(1)}, f32[4,1024,1024]{1,2,0:T(8,128)}) fusion(f32[4,1024,1024]{1,2,0:T(8,128)} %convolution_add_fusion.2), kind=kOutput, calls=%fused_computation.106.clone.1 | output fusion | flops 8389631 | bytes 33570816 | tf_op jit(solution)/shard_map/while/body/eval_jaxpr/sub | solution.py:80
  434.9 23.3 %fusion.128 = (bf16[4,1024,1024]{1,2,0:T(8,128)(2,1)S(1)}, f32[4,1024,1024]{1,2,0:T(8,128)}) fusion(f32[4,1024,1024]{1,2,0:T(8,128)} %get-tuple-element.193, f32[4,1024]{1,0:T(4,128)S(1)} %get-tuple-element.194, f32[4,1024,1024]{1,2,0:T(8,128)} %get-tuple-element.191, f32[4,1024]{1,0:T(4,128)S(1)} %get-tuple-element.192, ...), kind=kLoop, calls=%fused_computation.7.clone.1 | loop fusion | flops 25165824 | bytes 75530240 | tf_op jit(solution)/shard_map/while/body/eval_jaxpr/convert_element_type | solution.py:93
  504.0 18.6 %fusion.127 = (f32[4,1024]{1,0:T(4,128)S(1)}, f32[4,1024,1024]{1,2,0:T(8,128)}) fusion(f32[4,1024,1024]{1,2,0:T(8,128)} %convolution_add_fusion.2), kind=kOutput, calls=%fused_computation.106.clone.1 | output fusion | flops 8389631 | bytes 33570816 | tf_op jit(solution)/shard_map/while/body/eval_jaxpr/sub | solution.py:80
  522.6 14.3 multiply_reduce_fusion.4
  536.9 23.3 %fusion.128 = (bf16[4,1024,1024]{1,2,0:T(8,128)(2,1)S(1)}, f32[4,1024,1024]{1,2,0:T(8,128)}) fusion(f32[4,1024,1024]{1,2,0:T(8,128)} %get-tuple-element.193, f32[4,1024]{1,0:T(4,128)S(1)} %get-tuple-element.194, f32[4,1024,1024]{1,2,0:T(8,128)} %get-tuple-element.191, f32[4,1024]{1,0:T(4,128)S(1)} %get-tuple-element.192, ...), kind=kLoop, calls=%fused_computation.7.clone.1 | loop fusion | flops 25165824 | bytes 75530240 | tf_op jit(solution)/shard_map/while/body/eval_jaxpr/convert_element_type | solution.py:93
  606.1 18.6 %fusion.127 = (f32[4,1024]{1,0:T(4,128)S(1)}, f32[4,1024,1024]{1,2,0:T(8,128)}) fusion(f32[4,1024,1024]{1,2,0:T(8,128)} %convolution_add_fusion.2), kind=kOutput, calls=%fused_computation.106.clone.1 | output fusion | flops 8389631 | bytes 33570816 | tf_op jit(solution)/shard_map/while/body/eval_jaxpr/sub | solution.py:80
  639.0 23.3 %fusion.128 = (bf16[4,1024,1024]{1,2,0:T(8,128)(2,1)S(1)}, f32[4,1024,1024]{1,2,0:T(8,128)}) fusion(f32[4,1024,1024]{1,2,0:T(8,128)} %get-tuple-element.193, f32[4,1024]{1,0:T(4,128)S(1)} %get-tuple-element.194, f32[4,1024,1024]{1,2,0:T(8,128)} %get-tuple-element.191, f32[4,1024]{1,0:T(4,128)S(1)} %get-tuple-element.192, ...), kind=kLoop, calls=%fused_computation.7.clone.1 | loop fusion | flops 25165824 | bytes 75530240 | tf_op jit(solution)/shard_map/while/body/eval_jaxpr/convert_element_type | solution.py:93
  708.1 18.6 %fusion.127 = (f32[4,1024]{1,0:T(4,128)S(1)}, f32[4,1024,1024]{1,2,0:T(8,128)}) fusion(f32[4,1024,1024]{1,2,0:T(8,128)} %convolution_add_fusion.2), kind=kOutput, calls=%fused_computation.106.clone.1 | output fusion | flops 8389631 | bytes 33570816 | tf_op jit(solution)/shard_map/while/body/eval_jaxpr/sub | solution.py:80
  726.7 14.3 multiply_reduce_fusion.4
  741.0 23.3 %fusion.128 = (bf16[4,1024,1024]{1,2,0:T(8,128)(2,1)S(1)}, f32[4,1024,1024]{1,2,0:T(8,128)}) fusion(f32[4,1024,1024]{1,2,0:T(8,128)} %get-tuple-element.193, f32[4,1024]{1,0:T(4,128)S(1)} %get-tuple-element.194, f32[4,1024,1024]{1,2,0:T(8,128)} %get-tuple-element.191, f32[4,1024]{1,0:T(4,128)S(1)} %get-tuple-element.192, ...), kind=kLoop, calls=%fused_computation.7.clone.1 | loop fusion | flops 25165824 | bytes 75530240 | tf_op jit(solution)/shard_map/while/body/eval_jaxpr/convert_element_type | solution.py:93
  810.2 18.6 %fusion.127 = (f32[4,1024]{1,0:T(4,128)S(1)}, f32[4,1024,1024]{1,2,0:T(8,128)}) fusion(f32[4,1024,1024]{1,2,0:T(8,128)} %convolution_add_fusion.2), kind=kOutput, calls=%fused_computation.106.clone.1 | output fusion | flops 8389631 | bytes 33570816 | tf_op jit(solution)/shard_map/while/body/eval_jaxpr/sub | solution.py:80
  843.1 23.3 %fusion.128 = (bf16[4,1024,1024]{1,2,0:T(8,128)(2,1)S(1)}, f32[4,1024,1024]{1,2,0:T(8,128)}) fusion(f32[4,1024,1024]{1,2,0:T(8,128)} %get-tuple-element.193, f32[4,1024]{1,0:T(4,128)S(1)} %get-tuple-element.194, f32[4,1024,1024]{1,2,0:T(8,128)} %get-tuple-element.191, f32[4,1024]{1,0:T(4,128)S(1)} %get-tuple-element.192, ...), kind=kLoop, calls=%fused_computation.7.clone.1 | loop fusion | flops 25165824 | bytes 75530240 | tf_op jit(solution)/shard_map/while/body/eval_jaxpr/convert_element_type | solution.py:93
  912.2 18.6 %fusion.127 = (f32[4,1024]{1,0:T(4,128)S(1)}, f32[4,1024,1024]{1,2,0:T(8,128)}) fusion(f32[4,1024,1024]{1,2,0:T(8,128)} %convolution_add_fusion.2), kind=kOutput, calls=%fused_computation.106.clone.1 | output fusion | flops 8389631 | bytes 33570816 | tf_op jit(solution)/shard_map/while/body/eval_jaxpr/sub | solution.py:80
  945.1 23.3 %fusion.128 = (bf16[4,1024,1024]{1,2,0:T(8,128)(2,1)S(1)}, f32[4,1024,1024]{1,2,0:T(8,128)}) fusion(f32[4,1024,1024]{1,2,0:T(8,128)} %get-tuple-element.193, f32[4,1024]{1,0:T(4,128)S(1)} %get-tuple-element.194, f32[4,1024,1024]{1,2,0:T(8,128)} %get-tuple-element.191, f32[4,1024]{1,0:T(4,128)S(1)} %get-tuple-element.192, ...), kind=kLoop, calls=%fused_computation.7.clone.1 | loop fusion | flops 25165824 | bytes 75530240 | tf_op jit(solution)/shard_map/while/body/eval_jaxpr/convert_element_type | solution.py:93
  1000.3 20.2 %copy.73 = f32[4,1024,1024]{2,0,1:T(4,128)} copy(f32[4,1024,1024]{1,2,0:T(8,128)} %get-tuple-element.51) | data formatting | bytes 33554432 | tf_op jit(solution)/shard_map/while | solution.py:107
  1028.3 364.2 %all-reduce.2 = bf16[4,1024,1024]{2,0,1:T(4,128)(2,1)} all-reduce(f32[4,1024,1024]{2,0,1:T(4,128)} %copy.73), channel_id=3, replica_groups=mesh['seq'=16,'head'=2] {'seq'}, use_global_device_ids=true, to_apply=%region_12.13.clone | all-reduce | flops 4194304 | bytes 25165824
  (146 shorter events, 564.0 us)
Async XLA Ops:
  7.2 154.0 %copy-start = (bf16[256,256]{1,0:T(8,128)(2,1)S(1)}, bf16[256,256]{1,0:T(8,128)(2,1)}, u32[]{:S(2)}) copy-start(bf16[256,256]{1,0:T(8,128)(2,1)} %param.27) | copy-start | bytes 393220
  7.2 8.8 copy-start.10
  7.2 8.9 copy-start.11
  7.2 9.0 copy-start.12
  7.2 9.1 copy-start.13
  7.2 156.8 %all-gather.2.cloned.1.call-start = ((), (), s32[]{:S(2)}) async-start(), calls=%async_computation.3 | async-start | bytes 8912896 | tf_op jit(solution)/shard_map/all_gather | solution.py:46
  9.7 149.0 %all-to-all-start = ((bf16[128,64,256]{2,1,0:T(8,128)(2,1)}), bf16[128,64,256]{2,1,0:T(8,128)(2,1)}, u32[]{:S(2)}, u32[]{:S(2)}) async-start(bf16[128,64,256]{2,1,0:T(8,128)(2,1)} %param.17), calls=%async_computation | async-start | bytes 8388608 | tf_op jit(solution)/shard_map/all_to_all | solution.py:65
  15.9 1421.3 %reduce-scatter.2.cloned.1.call-start = ((), (), s32[]{:S(2)}) async-start(), calls=%async_computation.4 | async-start | bytes 6291456 | tf_op jit(solution)/shard_map/reduce_scatter | solution.py:129
  16.5 12.9 copy-start.18
  16.5 13.0 copy-start.20
  30.7 10.5 copy-start.3
  30.7 10.5 copy-start.14
  30.7 10.5 copy-start.19
  39.1 22.8 %copy-start.8 = (f32[8,1024]{1,0:T(8,128)}, f32[8,1024]{1,0:T(8,128)S(1)}, u32[]{:S(2)}) copy-start(f32[8,1024]{1,0:T(8,128)S(1)} %add_rsqrt_fusion.1) | copy-start | bytes 98308
  41.2 16.8 %copy-start.4 = (f32[64,512]{1,0:T(8,128)}, f32[64,512]{1,0:T(8,128)S(1)}, u32[]{:S(2)}) copy-start(f32[64,512]{1,0:T(8,128)S(1)} %broadcast_multiply_fusion.2) | copy-start | bytes 393220
  1000.3 20.2 %copy-start.7 = (bf16[256,8,4,32]{0,3,2,1:T(8,128)(2,1)S(1)}, bf16[256,8,4,32]{0,3,2,1:T(8,128)(2,1)}, u32[]{:S(2)}) copy-start(bf16[256,8,4,32]{0,3,2,1:T(8,128)(2,1)} %copy.69) | copy-start | bytes 1572868
  1028.3 371.4 %copy-start.9 = (f32[8,1024]{1,0:T(8,128)S(1)}, f32[8,1024]{1,0:T(8,128)}, u32[]{:S(2)}) copy-start(f32[8,1024]{1,0:T(8,128)} %copy-done.8) | copy-start | bytes 98308
  1028.3 371.4 %copy-start.6 = (f32[64,512]{1,0:T(8,128)S(1)}, f32[64,512]{1,0:T(8,128)}, u32[]{:S(2)}) copy-start(f32[64,512]{1,0:T(8,128)} %fusion.60) | copy-start | bytes 393220
  1392.5 15.4 %copy-start.5 = (f32[64,512]{1,0:T(8,128)S(1)}, f32[64,512]{1,0:T(8,128)}, u32[]{:S(2)}) copy-start(f32[64,512]{1,0:T(8,128)} %copy-done.4) | copy-start | bytes 393220
  1392.5 15.4 %copy-start.16 = (f32[128]{0:T(128)S(1)}, f32[128]{0:T(128)}, u32[]{:S(2)}) copy-start(f32[128]{0:T(128)} %param.28) | copy-start | bytes 1540
  1392.5 15.4 %copy-start.17 = (bf16[128,8]{0,1:T(8,128)(2,1)S(1)}, bf16[128,8]{0,1:T(8,128)(2,1)}, u32[]{:S(2)}) copy-start(bf16[128,8]{0,1:T(8,128)(2,1)} %param.29) | copy-start | bytes 6148
  1396.2 10.1 all-to-all-start.1
  1425.2 12.0 copy-start.15
  1425.2 21.5 %copy-start.1 = (bf16[256,256]{1,0:T(8,128)(2,1)S(1)}, bf16[256,256]{1,0:T(8,128)(2,1)}, u32[]{:S(2)}) copy-start(bf16[256,256]{1,0:T(8,128)(2,1)} %param.27) | copy-start | bytes 393220
  (1 other events, 8.4 us)
Sparse Core Ops, SparseCore 0:
  10.2 136.0 all-gather.1
  1028.4 54.2 reduce-scatter.1
where the time goes:
time: 1470 us; the launch traced here: 1450 us
  matrix products  507 us (34%)
  other arithmetic  376 us (26%)
  blocking collectives  364 us (25%)
  waiting for transfers between devices  98.3 us (7%)
  local copies, waits for them, and re-layouts  72.1 us (5%)
  between operations  15.5 us (1%)
    unnamed x1, blocking collectives  364 us
    convert_element_type x8, other arithmetic, row_reverse_step(): score_low = score_grad.astype(jnp.bfloat16)  180 us
    sub x8, other arithmetic, row_reverse_step(): probs = jax.nn.softmax(logits, axis=-1)  149 us
    dot_general x8, matrix products, row_reverse_step(): jnp.einsum('ihd,jhd->hij', attended_grad, vals_row, preferred_element_typ...  114 us
    dot_general x8, matrix products, row_reverse_step(): jnp.einsum('ihd,jhd->hij', query_row, keys_row, preferred_element_type=jn...  112 us
    dot_general x8, matrix products, row_reverse_step(): jnp.einsum('hij,ihd->jhd', probs_low, attended_grad, preferred_element_ty...  104 us
    dot_general x8, matrix products, row_reverse_step(): jnp.einsum('hij,jhd->ihd', probs_low, vals_row, preferred_element_type=jn...  103 us
    all_to_all x1, waiting for transfers between devices, per_device(): lax.all_to_all(upstream_derivative_tensor, 'seq', split_axis=0, concat_ax...  91.8 us
  transfers between devices with their start and end apart: 4, of which 2 were waited for; matrix products, arithmetic and copies ran while one was open for 6% of the time, Pallas kernels for 0%

commit v1 on v0

--- a/solution.py
+++ b/solution.py
@@ -62,8 +62,14 @@
     gate_shift = lax.dynamic_slice_in_dim(gate_offset_bias, first_col, head_width, 0)
     gate = jax.nn.sigmoid(project(sigmoid_projection_matrix) + gate_shift).reshape(head_shape)
     out_rows = lax.dynamic_slice_in_dim(final_projection_matrix, first_col, head_width, 0)
-    row_grads = lax.all_to_all(
-        upstream_derivative_tensor, "seq", split_axis=0, concat_axis=1, tiled=True
+    row_grads = jnp.concatenate(
+        lax.all_to_all(
+            jnp.stack(jnp.split(upstream_derivative_tensor, lax.axis_size("seq"), axis=0)),
+            "seq",
+            0,
+            0,
+        ),
+        axis=1,
     )
     gated_grad = jnp.einsum(
         "src,wc->srw", row_grads, out_rows, preferred_element_type=jnp.float32

time: 1470 us -> 1480 us (level)
  local copies, waits for them, and re-layouts: 72.1 us -> 98.3 us
  waiting for transfers between devices: 98.3 us -> 82.1 us
    unnamed x53 -> x68, local copies, waits for them, and re-layouts: 45.5 us -> 69.9 us
    all_to_all x1, waiting for transfers between devices: 91.8 us -> 75.6 us  [per_device(): lax.all_to_all(jnp.stack(jnp.split(upstream_derivative_tensor, lax.axis_s...]
  transfers between devices with their start and end apart: 4 -> 4, of which waited for: 2 -> 2; matrix products, arithmetic and copies ran while one was open for 6% -> 8% of each run, Pallas kernels for 0% -> 0%
where the time goes in v1:
time: 1480 us; the launch traced here: 1460 us
  matrix products  507 us (34%)
  other arithmetic  376 us (25%)
  blocking collectives  364 us (25%)
  local copies, waits for them, and re-layouts  98.3 us (7%)
  waiting for transfers between devices  82.1 us (6%)
  between operations  15.5 us (1%)
    unnamed x1, blocking collectives  364 us
    convert_element_type x8, other arithmetic, row_reverse_step(): score_low = score_grad.astype(jnp.bfloat16)  180 us
    sub x8, other arithmetic, row_reverse_step(): probs = jax.nn.softmax(logits, axis=-1)  149 us
    dot_general x8, matrix products, row_reverse_step(): jnp.einsum('ihd,jhd->hij', attended_grad, vals_row, preferred_element_typ...  114 us
    dot_general x8, matrix products, row_reverse_step(): jnp.einsum('ihd,jhd->hij', query_row, keys_row, preferred_element_type=jn...  112 us
    dot_general x8, matrix products, row_reverse_step(): jnp.einsum('hij,ihd->jhd', probs_low, attended_grad, preferred_element_ty...  104 us
    dot_general x8, matrix products, row_reverse_step(): jnp.einsum('hij,jhd->ihd', probs_low, vals_row, preferred_element_type=jn...  103 us
    all_to_all x1, waiting for transfers between devices, per_device(): lax.all_to_all(jnp.stack(jnp.split(upstream_derivative_tensor, lax.axis_s...  75.6 us
  transfers between devices with their start and end apart: 4, of which 2 were waited for; matrix products, arithmetic and copies ran while one was open for 8% of the time, Pallas kernels for 0%

profile of v1, /device:TPU:10, one launch (start us, length us, event | category | flops | bytes accessed | tf_op | source)
XLA Modules:
  0.0 1463.9 jit_solution(17102461964424623337)
XLA Ops:
  93.0 75.6 %all-to-all-done = bf16[16,8,64,256]{3,2,1,0:T(8,128)(2,1)} async-done(((bf16[16,8,64,256]{3,2,1,0:T(8,128)(2,1)}), bf16[16,8,64,256]{3,2,1,0:T(8,128)(2,1)}, u32[]{:S(2)}, u32[]{:S(2)}) %all-to-all-start) | async-done | bytes 4194336 | tf_op jit(solution)/shard_map/all_to_all | solution.py:66
  174.0 15.8 %copy.64 = f32[4,1024,1024]{1,2,0:T(8,128)} copy(bf16[4,1024,1024]{2,0,1:T(4,128)(2,1)} %all-gather.2.cloned.1.call-done) | data formatting | bytes 25165824
  189.8 820.5 %while.13 = (s32[]{:T(128)}, f32[4,1024,1024]{1,2,0:T(8,128)}, bf16[8,1024,4,128]{1,3,2,0:T(8,128)(2,1)}, bf16[8,1024,4,32]{1,3,2,0:T(8,128)(2,1)}, bf16[8,1024,...) while((s32[]{:T(128)}, f32[4,1024,1024]{1,2,0:T(8,128)}, ...), condition=%wide.region_6.7_spmd.clone, body=%wide.region_2.6_spmd.clone.sunk | while | flops 1692408832 | bytes 267244176 | solution.py:113
  213.8 18.6 %fusion.127 = (f32[4,1024]{1,0:T(4,128)S(1)}, f32[4,1024,1024]{1,2,0:T(8,128)}) fusion(f32[4,1024,1024]{1,2,0:T(8,128)} %convolution_add_fusion.2), kind=kOutput, calls=%fused_computation.122.clone.1 | output fusion | flops 8389631 | bytes 33570816 | tf_op jit(solution)/shard_map/while/body/eval_jaxpr/sub | solution.py:86
  246.7 17.3 %fusion.128 = (bf16[4,1024,1024]{1,2,0:T(8,128)(2,1)S(1)}, f32[4,1024,1024]{1,2,0:T(8,128)}) fusion(f32[4,1024,1024]{1,2,0:T(8,128)} %get-tuple-element.193, f32[4,1024]{1,0:T(4,128)S(1)} %get-tuple-element.194, f32[4,1024,1024]{1,2,0:T(8,128)} %get-tuple-element.191, f32[4,1024]{1,0:T(4,128)S(1)} %get-tuple-element.192, ...), kind=kLoop, calls=%fused_computation.7.clone.1 | loop fusion | flops 25165824 | bytes 75530240 | tf_op jit(solution)/shard_map/while/body/eval_jaxpr/convert_element_type | solution.py:99
  309.8 18.6 %fusion.127 = (f32[4,1024]{1,0:T(4,128)S(1)}, f32[4,1024,1024]{1,2,0:T(8,128)}) fusion(f32[4,1024,1024]{1,2,0:T(8,128)} %convolution_add_fusion.2), kind=kOutput, calls=%fused_computation.122.clone.1 | output fusion | flops 8389631 | bytes 33570816 | tf_op jit(solution)/shard_map/while/body/eval_jaxpr/sub | solution.py:86
  328.4 14.3 multiply_reduce_fusion.4
  342.7 23.3 %fusion.128 = (bf16[4,1024,1024]{1,2,0:T(8,128)(2,1)S(1)}, f32[4,1024,1024]{1,2,0:T(8,128)}) fusion(f32[4,1024,1024]{1,2,0:T(8,128)} %get-tuple-element.193, f32[4,1024]{1,0:T(4,128)S(1)} %get-tuple-element.194, f32[4,1024,1024]{1,2,0:T(8,128)} %get-tuple-element.191, f32[4,1024]{1,0:T(4,128)S(1)} %get-tuple-element.192, ...), kind=kLoop, calls=%fused_computation.7.clone.1 | loop fusion | flops 25165824 | bytes 75530240 | tf_op jit(solution)/shard_map/while/body/eval_jaxpr/convert_element_type | solution.py:99
  411.9 18.6 %fusion.127 = (f32[4,1024]{1,0:T(4,128)S(1)}, f32[4,1024,1024]{1,2,0:T(8,128)}) fusion(f32[4,1024,1024]{1,2,0:T(8,128)} %convolution_add_fusion.2), kind=kOutput, calls=%fused_computation.122.clone.1 | output fusion | flops 8389631 | bytes 33570816 | tf_op jit(solution)/shard_map/while/body/eval_jaxpr/sub | solution.py:86
  444.8 23.3 %fusion.128 = (bf16[4,1024,1024]{1,2,0:T(8,128)(2,1)S(1)}, f32[4,1024,1024]{1,2,0:T(8,128)}) fusion(f32[4,1024,1024]{1,2,0:T(8,128)} %get-tuple-element.193, f32[4,1024]{1,0:T(4,128)S(1)} %get-tuple-element.194, f32[4,1024,1024]{1,2,0:T(8,128)} %get-tuple-element.191, f32[4,1024]{1,0:T(4,128)S(1)} %get-tuple-element.192, ...), kind=kLoop, calls=%fused_computation.7.clone.1 | loop fusion | flops 25165824 | bytes 75530240 | tf_op jit(solution)/shard_map/while/body/eval_jaxpr/convert_element_type | solution.py:99
  513.9 18.6 %fusion.127 = (f32[4,1024]{1,0:T(4,128)S(1)}, f32[4,1024,1024]{1,2,0:T(8,128)}) fusion(f32[4,1024,1024]{1,2,0:T(8,128)} %convolution_add_fusion.2), kind=kOutput, calls=%fused_computation.122.clone.1 | output fusion | flops 8389631 | bytes 33570816 | tf_op jit(solution)/shard_map/while/body/eval_jaxpr/sub | solution.py:86
  532.5 14.3 multiply_reduce_fusion.4
  546.8 23.3 %fusion.128 = (bf16[4,1024,1024]{1,2,0:T(8,128)(2,1)S(1)}, f32[4,1024,1024]{1,2,0:T(8,128)}) fusion(f32[4,1024,1024]{1,2,0:T(8,128)} %get-tuple-element.193, f32[4,1024]{1,0:T(4,128)S(1)} %get-tuple-element.194, f32[4,1024,1024]{1,2,0:T(8,128)} %get-tuple-element.191, f32[4,1024]{1,0:T(4,128)S(1)} %get-tuple-element.192, ...), kind=kLoop, calls=%fused_computation.7.clone.1 | loop fusion | flops 25165824 | bytes 75530240 | tf_op jit(solution)/shard_map/while/body/eval_jaxpr/convert_element_type | solution.py:99
  616.0 18.6 %fusion.127 = (f32[4,1024]{1,0:T(4,128)S(1)}, f32[4,1024,1024]{1,2,0:T(8,128)}) fusion(f32[4,1024,1024]{1,2,0:T(8,128)} %convolution_add_fusion.2), kind=kOutput, calls=%fused_computation.122.clone.1 | output fusion | flops 8389631 | bytes 33570816 | tf_op jit(solution)/shard_map/while/body/eval_jaxpr/sub | solution.py:86
  648.9 23.3 %fusion.128 = (bf16[4,1024,1024]{1,2,0:T(8,128)(2,1)S(1)}, f32[4,1024,1024]{1,2,0:T(8,128)}) fusion(f32[4,1024,1024]{1,2,0:T(8,128)} %get-tuple-element.193, f32[4,1024]{1,0:T(4,128)S(1)} %get-tuple-element.194, f32[4,1024,1024]{1,2,0:T(8,128)} %get-tuple-element.191, f32[4,1024]{1,0:T(4,128)S(1)} %get-tuple-element.192, ...), kind=kLoop, calls=%fused_computation.7.clone.1 | loop fusion | flops 25165824 | bytes 75530240 | tf_op jit(solution)/shard_map/while/body/eval_jaxpr/convert_element_type | solution.py:99
  718.1 18.6 %fusion.127 = (f32[4,1024]{1,0:T(4,128)S(1)}, f32[4,1024,1024]{1,2,0:T(8,128)}) fusion(f32[4,1024,1024]{1,2,0:T(8,128)} %convolution_add_fusion.2), kind=kOutput, calls=%fused_computation.122.clone.1 | output fusion | flops 8389631 | bytes 33570816 | tf_op jit(solution)/shard_map/while/body/eval_jaxpr/sub | solution.py:86
  736.7 14.3 multiply_reduce_fusion.4
  751.0 23.3 %fusion.128 = (bf16[4,1024,1024]{1,2,0:T(8,128)(2,1)S(1)}, f32[4,1024,1024]{1,2,0:T(8,128)}) fusion(f32[4,1024,1024]{1,2,0:T(8,128)} %get-tuple-element.193, f32[4,1024]{1,0:T(4,128)S(1)} %get-tuple-element.194, f32[4,1024,1024]{1,2,0:T(8,128)} %get-tuple-element.191, f32[4,1024]{1,0:T(4,128)S(1)} %get-tuple-element.192, ...), kind=kLoop, calls=%fused_computation.7.clone.1 | loop fusion | flops 25165824 | bytes 75530240 | tf_op jit(solution)/shard_map/while/body/eval_jaxpr/convert_element_type | solution.py:99
  820.1 18.6 %fusion.127 = (f32[4,1024]{1,0:T(4,128)S(1)}, f32[4,1024,1024]{1,2,0:T(8,128)}) fusion(f32[4,1024,1024]{1,2,0:T(8,128)} %convolution_add_fusion.2), kind=kOutput, calls=%fused_computation.122.clone.1 | output fusion | flops 8389631 | bytes 33570816 | tf_op jit(solution)/shard_map/while/body/eval_jaxpr/sub | solution.py:86
  853.0 23.3 %fusion.128 = (bf16[4,1024,1024]{1,2,0:T(8,128)(2,1)S(1)}, f32[4,1024,1024]{1,2,0:T(8,128)}) fusion(f32[4,1024,1024]{1,2,0:T(8,128)} %get-tuple-element.193, f32[4,1024]{1,0:T(4,128)S(1)} %get-tuple-element.194, f32[4,1024,1024]{1,2,0:T(8,128)} %get-tuple-element.191, f32[4,1024]{1,0:T(4,128)S(1)} %get-tuple-element.192, ...), kind=kLoop, calls=%fused_computation.7.clone.1 | loop fusion | flops 25165824 | bytes 75530240 | tf_op jit(solution)/shard_map/while/body/eval_jaxpr/convert_element_type | solution.py:99
  922.2 18.6 %fusion.127 = (f32[4,1024]{1,0:T(4,128)S(1)}, f32[4,1024,1024]{1,2,0:T(8,128)}) fusion(f32[4,1024,1024]{1,2,0:T(8,128)} %convolution_add_fusion.2), kind=kOutput, calls=%fused_computation.122.clone.1 | output fusion | flops 8389631 | bytes 33570816 | tf_op jit(solution)/shard_map/while/body/eval_jaxpr/sub | solution.py:86
  955.1 23.3 %fusion.128 = (bf16[4,1024,1024]{1,2,0:T(8,128)(2,1)S(1)}, f32[4,1024,1024]{1,2,0:T(8,128)}) fusion(f32[4,1024,1024]{1,2,0:T(8,128)} %get-tuple-element.193, f32[4,1024]{1,0:T(4,128)S(1)} %get-tuple-element.194, f32[4,1024,1024]{1,2,0:T(8,128)} %get-tuple-element.191, f32[4,1024]{1,0:T(4,128)S(1)} %get-tuple-element.192, ...), kind=kLoop, calls=%fused_computation.7.clone.1 | loop fusion | flops 25165824 | bytes 75530240 | tf_op jit(solution)/shard_map/while/body/eval_jaxpr/convert_element_type | solution.py:99
  1010.3 20.2 %copy.73 = f32[4,1024,1024]{2,0,1:T(4,128)} copy(f32[4,1024,1024]{1,2,0:T(8,128)} %get-tuple-element.51) | data formatting | bytes 33554432 | tf_op jit(solution)/shard_map/while | solution.py:113
  1038.3 364.3 %all-reduce.2 = bf16[4,1024,1024]{2,0,1:T(4,128)(2,1)} all-reduce(f32[4,1024,1024]{2,0,1:T(4,128)} %copy.73), channel_id=3, replica_groups=mesh['seq'=16,'head'=2] {'seq'}, use_global_device_ids=true, to_apply=%region_12.13.clone | all-reduce | flops 4194304 | bytes 25165824
  (162 shorter events, 590.1 us)
Async XLA Ops:
  7.2 163.9 %copy-start = (bf16[256,256]{1,0:T(8,128)(2,1)S(1)}, bf16[256,256]{1,0:T(8,128)(2,1)}, u32[]{:S(2)}) copy-start(bf16[256,256]{1,0:T(8,128)(2,1)} %param.27) | copy-start | bytes 393220
  7.2 166.8 %all-gather.2.cloned.1.call-start = ((), (), s32[]{:S(2)}) async-start(), calls=%async_computation.3 | async-start | bytes 8912896 | tf_op jit(solution)/shard_map/all_gather | solution.py:46
  9.6 33.3 %copy-start.10 = (bf16[256,256]{1,0:T(8,128)(2,1)S(1)}, bf16[256,256]{1,0:T(8,128)(2,1)}, u32[]{:S(2)}) copy-start(bf16[256,256]{1,0:T(8,128)(2,1)} %param.25) | copy-start | bytes 393220
  11.3 31.7 %copy-start.11 = (bf16[256,256]{1,0:T(8,128)(2,1)S(1)}, bf16[256,256]{1,0:T(8,128)(2,1)}, u32[]{:S(2)}) copy-start(bf16[256,256]{1,0:T(8,128)(2,1)} %param.22) | copy-start | bytes 393220
  11.3 31.8 %copy-start.12 = (bf16[256,256]{1,0:T(8,128)(2,1)S(1)}, bf16[256,256]{1,0:T(8,128)(2,1)}, u32[]{:S(2)}) copy-start(bf16[256,256]{1,0:T(8,128)(2,1)} %param.24) | copy-start | bytes 393220
  13.0 30.2 %copy-start.13 = (bf16[256,256]{1,0:T(8,128)(2,1)S(1)}, bf16[256,256]{1,0:T(8,128)(2,1)}, u32[]{:S(2)}) copy-start(bf16[256,256]{1,0:T(8,128)(2,1)} %param.23) | copy-start | bytes 393220
  36.5 132.1 %all-to-all-start = ((bf16[16,8,64,256]{3,2,1,0:T(8,128)(2,1)}), bf16[16,8,64,256]{3,2,1,0:T(8,128)(2,1)}, u32[]{:S(2)}, u32[]{:S(2)}) async-start(bf16[16,8,64,256]{3,2,1,0:T(8,128)(2,1)} %bitcast_dynamic-update-slice_fusion), calls=%async_computation | async-start | bytes 8388608 | tf_op jit(solution)/shard_map/all_to_all | solution.py:66
  42.8 1404.4 %reduce-scatter.2.cloned.1.call-start = ((), (), s32[]{:S(2)}) async-start(), calls=%async_computation.4 | async-start | bytes 6291456 | tf_op jit(solution)/shard_map/reduce_scatter | solution.py:135
  43.3 12.2 copy-start.18
  43.3 12.2 copy-start.20
  56.8 10.5 copy-start.3
  56.8 10.5 copy-start.14
  56.8 10.5 copy-start.19
  65.3 22.8 %copy-start.8 = (f32[8,1024]{1,0:T(8,128)}, f32[8,1024]{1,0:T(8,128)S(1)}, u32[]{:S(2)}) copy-start(f32[8,1024]{1,0:T(8,128)S(1)} %add_rsqrt_fusion.1) | copy-start | bytes 98308
  67.4 16.8 %copy-start.4 = (f32[64,512]{1,0:T(8,128)}, f32[64,512]{1,0:T(8,128)S(1)}, u32[]{:S(2)}) copy-start(f32[64,512]{1,0:T(8,128)S(1)} %broadcast_multiply_fusion.2) | copy-start | bytes 393220
  1010.3 20.2 %copy-start.7 = (bf16[256,8,4,32]{0,3,2,1:T(8,128)(2,1)S(1)}, bf16[256,8,4,32]{0,3,2,1:T(8,128)(2,1)}, u32[]{:S(2)}) copy-start(bf16[256,8,4,32]{0,3,2,1:T(8,128)(2,1)} %copy.69) | copy-start | bytes 1572868
  1038.2 371.5 %copy-start.9 = (f32[8,1024]{1,0:T(8,128)S(1)}, f32[8,1024]{1,0:T(8,128)}, u32[]{:S(2)}) copy-start(f32[8,1024]{1,0:T(8,128)} %copy-done.8) | copy-start | bytes 98308
  1038.2 371.5 %copy-start.6 = (f32[64,512]{1,0:T(8,128)S(1)}, f32[64,512]{1,0:T(8,128)}, u32[]{:S(2)}) copy-start(f32[64,512]{1,0:T(8,128)} %fusion.60) | copy-start | bytes 393220
  1402.5 15.4 %copy-start.5 = (f32[64,512]{1,0:T(8,128)S(1)}, f32[64,512]{1,0:T(8,128)}, u32[]{:S(2)}) copy-start(f32[64,512]{1,0:T(8,128)} %copy-done.4) | copy-start | bytes 393220
  1402.5 15.4 %copy-start.16 = (f32[128]{0:T(128)S(1)}, f32[128]{0:T(128)}, u32[]{:S(2)}) copy-start(f32[128]{0:T(128)} %param.28) | copy-start | bytes 1540
  1402.5 15.4 %copy-start.17 = (bf16[128,8]{0,1:T(8,128)(2,1)S(1)}, bf16[128,8]{0,1:T(8,128)(2,1)}, u32[]{:S(2)}) copy-start(bf16[128,8]{0,1:T(8,128)(2,1)} %param.29) | copy-start | bytes 6148
  1406.2 10.1 all-to-all-start.1
  1435.2 12.0 copy-start.15
  1435.2 21.5 %copy-start.1 = (bf16[256,256]{1,0:T(8,128)(2,1)S(1)}, bf16[256,256]{1,0:T(8,128)(2,1)}, u32[]{:S(2)}) copy-start(bf16[256,256]{1,0:T(8,128)(2,1)} %param.27) | copy-start | bytes 393220
  (1 other events, 8.4 us)
Sparse Core Ops, SparseCore 0:
  10.1 130.4 all-gather.1
  1038.4 54.3 reduce-scatter.1
